TPU v7x, 32 devices: a whole 2x2x4 slice. The times are simulated.
32 devices in a mesh: dp: 16 (over z, y, core), mlp: 2 (over x).
Axes of the slice: x: 2, y: 2, z: 4, core: 2. Of those that a mesh axis runs over, the one named last changes fastest.
Arguments:
- tokens: bfloat16 [2, 20480, 768], P(None, ('dp', 'mlp')), may hold values from -6 to 6
- cotangent: bfloat16 [2, 20480, 768], P(None, ('dp', 'mlp')), may hold values from -6 to 6
- lengths: int32 [2, 32, 4], P(None, ('dp', 'mlp')), may hold values from 0 to 577, as said below
- buckets: int32 [2, 32], P(None, ('dp', 'mlp')), may hold values from 0 to 2, as said below
- pos_table: bfloat16 [875, 768], replicated, may hold values from -6 to 6
- prompts: bfloat16 [50, 768], replicated, may hold values from -6 to 6
- norm1_gain: bfloat16 [768], replicated, may hold values from 0.25 to 1.75
- norm1_bias: bfloat16 [768], replicated, may hold values from -3 to 3
- qkv_weight: bfloat16 [768, 2304], P(('dp', 'mlp')), may hold values from -0.21875 to 0.21875
- q_bias: bfloat16 [768], replicated, may hold values from -3 to 3
- v_bias: bfloat16 [768], replicated, may hold values from -3 to 3
- out_weight: bfloat16 [768, 768], P(('dp', 'mlp')), may hold values from -2 to 2
- out_bias: bfloat16 [768], replicated, may hold values from -3 to 3
- norm2_gain: bfloat16 [768], replicated, may hold values from 0.25 to 1.75
- norm2_bias: bfloat16 [768], replicated, may hold values from -3 to 3
- up_weight: bfloat16 [768, 3072], P('dp', 'mlp'), may hold values from -0.21875 to 0.21875
- up_bias: bfloat16 [3072], P('mlp'), may hold values from -3 to 3
- down_weight: bfloat16 [3072, 768], P('mlp', 'dp'), may hold values from -0.109375 to 0.109375
- down_bias: bfloat16 [768], replicated, may hold values from -3 to 3
Outputs:
- output: bfloat16 [2, 20480, 768], P(None, ('dp', 'mlp'))
- input_grad: float32 [2, 20480, 768], P(None, ('dp', 'mlp'))
- prompts_grad: float32 [50, 768], replicated
- norm1_gain_grad: float32 [768], replicated
- norm1_bias_grad: float32 [768], replicated
- qkv_weight_grad: float32 [768, 2304], P(('dp', 'mlp'))
- q_bias_grad: float32 [768], replicated
- v_bias_grad: float32 [768], replicated
- out_weight_grad: float32 [768, 768], P(('dp', 'mlp'))
- out_bias_grad: float32 [768], replicated
- norm2_gain_grad: float32 [768], replicated
- norm2_bias_grad: float32 [768], replicated
- up_weight_grad: float32 [768, 3072], P('dp', 'mlp')
- up_bias_grad: float32 [3072], P('mlp')
- down_weight_grad: float32 [3072, 768], P('mlp', 'dp')
- down_bias_grad: float32 [768], replicated
Inputs may be any that keep to these rules, and one draw needn't show every extreme that they name: `lengths`: in every buffer the first min(4, 640 // (50 + c)) slots hold c, the image tokens of the buffer's bucket (101, 197, 577 for buckets 0, 1, 2), and the others 0. `buckets`: every micro-batch has buffers of bucket 0 and of bucket 2.
All inputs are finite; a program needn't handle non-finite values.
Results may differ from a plain program's by a relative error of at most 0.012.
Values may be sent and summed in bfloat16 or wider, within the bound.
No kernel may reach another device: no remote copies, remote signals or barrier semaphores. Data moves between devices by JAX's collectives and lax.ppermute only.
A program may use at most 320 MiB of HBM per device.

v0:
```python
import math

import jax
import jax.numpy as jnp
from jax import lax
from jax.sharding import PartitionSpec as P

D = 768
HEADS = 12
HEAD_DIM = 64
PROMPTS = 50
LEN_LOW = 101
LEN_MID = 197
TABLE = 875
SLOTS = 4
ROWS = 640


epsilon = 1e-06
masked_score = -1e30
highest = lax.Precision.HIGHEST
pdf_scale = 0.3989422804014327
erf_scale = 0.7071067811865476


def layout(slot_lengths, bucket_id, row_total):
    sizes_used = jnp.where(slot_lengths > 0, slot_lengths + PROMPTS, 0)
    seq_ends = jnp.cumsum(sizes_used)
    seq_starts = seq_ends - sizes_used
    row_ids = jnp.arange(row_total, dtype=jnp.int32)
    sequence = jnp.sum((seq_ends[None, :] <= row_ids[:, None]).astype(jnp.int32), axis=1)
    slot_ids = jnp.arange(SLOTS, dtype=jnp.int32)
    own_start = jnp.sum(
        jnp.where(sequence[:, None] == slot_ids[None, :], seq_starts[None, :], 0), axis=1
    )
    position = row_ids - own_start
    inside = sequence < SLOTS
    is_prompt = inside & (position < PROMPTS)
    is_image = inside & (position >= PROMPTS)
    table_start = jnp.where(
        bucket_id == 0, 0, jnp.where(bucket_id == 1, LEN_LOW, LEN_LOW + LEN_MID)
    ).astype(jnp.int32)
    table_index = jnp.clip(table_start + position - PROMPTS, 0, TABLE - 1)
    prompt_index = jnp.clip(position, 0, PROMPTS - 1)
    return (sequence, inside, is_prompt, is_image, table_index, prompt_index)


def norm_apply(values_in, norm_gain, norm_shift):
    average = jnp.mean(values_in, axis=-1, keepdims=True)
    centred = values_in - average
    variance = jnp.mean(centred * centred, axis=-1, keepdims=True)
    return centred * lax.rsqrt(variance + epsilon) * norm_gain + norm_shift


def gelu_slope(hidden_pre):
    return (
        0.5 * (1.0 + lax.erf(hidden_pre * erf_scale))
        + hidden_pre * jnp.exp(-0.5 * hidden_pre * hidden_pre) * pdf_scale
    )


def split_heads(qkv_buffer):
    row_total = qkv_buffer.shape[0]
    queries = qkv_buffer[:, :D].reshape(row_total, HEADS, HEAD_DIM)
    key_rows = qkv_buffer[:, D : 2 * D].reshape(row_total, HEADS, HEAD_DIM)
    value_rows = qkv_buffer[:, 2 * D :].reshape(row_total, HEADS, HEAD_DIM)
    return (queries, key_rows, value_rows)


def masked_scores(queries, key_rows, sequence):
    scores = jnp.einsum(
        "qhd,khd->hqk", queries, key_rows, preferred_element_type=jnp.float32
    ) / math.sqrt(HEAD_DIM)
    same_seq = sequence[:, None] == sequence[None, :]
    return jnp.where(same_seq[None], scores, masked_score)


def attend(inputs):
    qkv_buffer, sequence = inputs
    row_total = qkv_buffer.shape[0]
    queries, key_rows, value_rows = split_heads(qkv_buffer)
    scores = masked_scores(queries, key_rows, sequence)
    row_max = jnp.max(scores, axis=-1, keepdims=True)
    expon = jnp.exp(scores - row_max)
    totals = jnp.sum(expon, axis=-1, keepdims=True)
    weights_soft = (expon / totals).astype(jnp.bfloat16)
    log_total = (row_max + jnp.log(totals))[..., 0]
    attended = jnp.einsum(
        "hqk,khd->qhd", weights_soft, value_rows, preferred_element_type=jnp.float32
    )
    return (attended.reshape(row_total, D).astype(jnp.bfloat16), log_total)


def attend_back(inputs):
    qkv_buffer, sequence, log_total, grad_attended = inputs
    row_total = qkv_buffer.shape[0]
    queries, key_rows, value_rows = split_heads(qkv_buffer)
    scores = masked_scores(queries, key_rows, sequence)
    weights_soft = jnp.exp(scores - log_total[..., None])
    grad_heads = grad_attended.reshape(row_total, HEADS, HEAD_DIM)
    grad_weights = jnp.einsum(
        "qhd,khd->hqk", grad_heads, value_rows, preferred_element_type=jnp.float32
    )
    inner = jnp.sum(weights_soft * grad_weights, axis=-1, keepdims=True)
    grad_scores = (weights_soft * (grad_weights - inner)).astype(jnp.bfloat16)
    grad_queries = jnp.einsum(
        "hqk,khd->qhd", grad_scores, key_rows, preferred_element_type=jnp.float32
    ) / math.sqrt(HEAD_DIM)
    grad_keys = jnp.einsum(
        "hqk,qhd->khd", grad_scores, queries, preferred_element_type=jnp.float32
    ) / math.sqrt(HEAD_DIM)
    grad_values = jnp.einsum(
        "hqk,qhd->khd",
        weights_soft.astype(jnp.bfloat16),
        grad_heads,
        preferred_element_type=jnp.float32,
    )
    joined = jnp.concatenate(
        [
            grad_queries.reshape(row_total, D),
            grad_keys.reshape(row_total, D),
            grad_values.reshape(row_total, D),
        ],
        axis=1,
    )
    return joined.astype(jnp.bfloat16)


def per_device(
    tokens,
    cotangent,
    lengths,
    buckets,
    pos_table,
    prompts,
    norm1_gain,
    norm1_bias,
    qkv_weight,
    q_bias,
    v_bias,
    out_weight,
    out_bias,
    norm2_gain,
    norm2_bias,
    up_weight,
    up_bias,
    down_weight,
    down_bias,
):
    micro_count = tokens.shape[0]
    local_rows = tokens.shape[1]
    buffer_count = lengths.shape[1]
    qkv_full, out_full = (
        lax.all_gather(qkv_weight, ("dp", "mlp"), axis=0, tiled=True),
        lax.all_gather(out_weight, ("dp", "mlp"), axis=0, tiled=True),
    )
    up_rows, down_cols = (
        lax.all_gather(up_weight, "dp", axis=0, tiled=True),
        lax.all_gather(down_weight, "dp", axis=1, tiled=True),
    )
    up_use, down_use, up_shift_use = (up_rows, down_cols, up_bias)
    prompt_rows = prompts.astype(jnp.float32)
    table_rows = pos_table.astype(jnp.float32)
    gain_one = norm1_gain.astype(jnp.float32)
    shift_one = norm1_bias.astype(jnp.float32)
    gain_two = norm2_gain.astype(jnp.float32)
    shift_two = norm2_bias.astype(jnp.float32)
    out_shift = out_bias.astype(jnp.float32)
    down_shift = down_bias.astype(jnp.float32)
    up_shift = up_shift_use.astype(jnp.float32)
    qkv_offset = jnp.concatenate(
        [q_bias.astype(jnp.float32), jnp.zeros((D,), jnp.float32), v_bias.astype(jnp.float32)]
    )
    mlp_size = lax.axis_size("mlp")
    hidden_local = up_use.shape[1]
    grad_qkv = jnp.zeros(qkv_full.shape, jnp.float32)
    grad_out = jnp.zeros(out_full.shape, jnp.float32)
    grad_up = jnp.zeros(up_use.shape, jnp.float32)
    grad_down = jnp.zeros(down_use.shape, jnp.float32)
    grad_up_shift = jnp.zeros((hidden_local,), jnp.float32)
    grad_prompts = jnp.zeros((PROMPTS, D), jnp.float32)
    grad_gain_one = jnp.zeros((D,), jnp.float32)
    grad_shift_one = jnp.zeros((D,), jnp.float32)
    grad_query_shift = jnp.zeros((D,), jnp.float32)
    grad_value_shift = jnp.zeros((D,), jnp.float32)
    grad_out_shift = jnp.zeros((D,), jnp.float32)
    grad_gain_two = jnp.zeros((D,), jnp.float32)
    grad_shift_two = jnp.zeros((D,), jnp.float32)
    grad_down_shift = jnp.zeros((D,), jnp.float32)
    outputs = []
    input_grads = []
    for micro_step in range(micro_count):
        sequence, inside, is_prompt, is_image, table_index, prompt_index = jax.vmap(
            lambda slot_lengths, bucket_id: layout(slot_lengths, bucket_id, ROWS)
        )(lengths[micro_step], buckets[micro_step])
        sequence = sequence.reshape(local_rows)
        inside = inside.reshape(local_rows)
        is_prompt = is_prompt.reshape(local_rows)
        is_image = is_image.reshape(local_rows)
        table_index = table_index.reshape(local_rows)
        prompt_index = prompt_index.reshape(local_rows)
        image_rows = tokens[micro_step].astype(jnp.float32)
        start_rows = jnp.where(
            is_prompt[:, None],
            jnp.take(prompt_rows, prompt_index, axis=0),
            jnp.where(
                is_image[:, None], image_rows + jnp.take(table_rows, table_index, axis=0), 0.0
            ),
        )
        normed = norm_apply(start_rows, gain_one, shift_one).astype(jnp.bfloat16)
        qkv_rows = (
            jnp.dot(normed, qkv_full, preferred_element_type=jnp.float32) + qkv_offset
        ).astype(jnp.bfloat16)
        qkv_buffers = qkv_rows.reshape(buffer_count, ROWS, 3 * D)
        seq_buffers = sequence.reshape(buffer_count, ROWS)
        attended, log_total = lax.map(attend, (qkv_buffers, seq_buffers))
        attended = attended.reshape(local_rows, D)
        first_sum = (
            start_rows + jnp.dot(attended, out_full, preferred_element_type=jnp.float32) + out_shift
        )
        normed_two = norm_apply(first_sum, gain_two, shift_two).astype(jnp.bfloat16)
        gathered_piece = lax.all_gather(normed_two, "mlp", axis=0, tiled=True)
        pre_part = jnp.dot(gathered_piece, up_use, preferred_element_type=jnp.float32) + up_shift
        activated = jax.nn.gelu(pre_part, approximate=False).astype(jnp.bfloat16)
        branch = lax.psum_scatter(
            jnp.dot(activated, down_use, preferred_element_type=jnp.float32).astype(jnp.bfloat16),
            "mlp",
            scatter_dimension=0,
            tiled=True,
        ).astype(jnp.float32)
        second_sum = first_sum + branch + down_shift
        valid_rows = inside[:, None].astype(jnp.float32)
        outputs.append((second_sum * valid_rows).astype(jnp.bfloat16))
        grad_two = cotangent[micro_step].astype(jnp.float32) * valid_rows
        grad_branch = grad_two.astype(jnp.bfloat16)
        grad_down_shift = grad_down_shift + jnp.sum(grad_two, axis=0)
        spread_gathered_piece = lax.all_gather(grad_branch, "mlp", axis=0, tiled=True)
        grad_act_part = jnp.einsum(
            "rd,fd->rf", spread_gathered_piece, down_use, preferred_element_type=jnp.float32
        )
        grad_part = (grad_act_part * gelu_slope(pre_part)).astype(jnp.bfloat16)
        down_total = jnp.einsum(
            "rf,rd->fd", activated, spread_gathered_piece, preferred_element_type=jnp.float32
        )
        grad_down = grad_down + down_total
        grad_normed = lax.psum_scatter(
            jnp.einsum("rf,df->rd", grad_part, up_use, preferred_element_type=jnp.float32).astype(
                jnp.bfloat16
            ),
            "mlp",
            scatter_dimension=0,
            tiled=True,
        ).astype(jnp.float32)
        grad_up = grad_up + jnp.einsum(
            "rd,rf->df", gathered_piece, grad_part, preferred_element_type=jnp.float32
        )
        grad_up_shift = grad_up_shift + jnp.sum(grad_part.astype(jnp.float32), axis=0)
        unused_two, pull_two = jax.vjp(norm_apply, first_sum, gain_two, shift_two)
        grad_first_part, grad_gain_part, grad_shift_part = pull_two(grad_normed)
        grad_gain_two = grad_gain_two + grad_gain_part
        grad_shift_two = grad_shift_two + grad_shift_part
        grad_one = grad_two + grad_first_part
        grad_out_shift = grad_out_shift + jnp.sum(grad_one, axis=0)
        grad_att = grad_one.astype(jnp.bfloat16)
        grad_out = grad_out + jnp.einsum(
            "rd,re->de", attended, grad_att, preferred_element_type=jnp.float32
        )
        grad_attended = jnp.einsum(
            "re,de->rd", grad_att, out_full, preferred_element_type=jnp.float32
        ).astype(jnp.bfloat16)
        grad_qkv_rows = lax.map(
            attend_back,
            (qkv_buffers, seq_buffers, log_total, grad_attended.reshape(buffer_count, ROWS, D)),
        )
        grad_qkv_rows = grad_qkv_rows.reshape(local_rows, 3 * D)
        grad_qkv = grad_qkv + jnp.einsum(
            "rd,re->de", normed, grad_qkv_rows, preferred_element_type=jnp.float32
        )
        column_sums = jnp.sum(grad_qkv_rows.astype(jnp.float32), axis=0)
        grad_query_shift = grad_query_shift + column_sums[:D]
        grad_value_shift = grad_value_shift + column_sums[2 * D :]
        grad_normed_one = jnp.einsum(
            "re,de->rd", grad_qkv_rows, qkv_full, preferred_element_type=jnp.float32
        )
        unused_one, pull_one = jax.vjp(norm_apply, start_rows, gain_one, shift_one)
        grad_start_part, grad_gain_part, grad_shift_part = pull_one(grad_normed_one)
        grad_gain_one = grad_gain_one + grad_gain_part
        grad_shift_one = grad_shift_one + grad_shift_part
        grad_zero = grad_one + grad_start_part
        input_grads.append(jnp.where(is_image[:, None], grad_zero, 0.0))
        prompt_hits = (
            (prompt_index[:, None] == jnp.arange(PROMPTS, dtype=jnp.int32)[None, :])
            & is_prompt[:, None]
        ).astype(jnp.float32)
        grad_prompts = grad_prompts + jnp.einsum(
            "rp,rd->pd", prompt_hits, grad_zero, precision=highest
        )
    qkv_weight_grad, out_weight_grad = (
        lax.psum_scatter(grad_qkv, ("dp", "mlp"), scatter_dimension=0, tiled=True),
        lax.psum_scatter(grad_out, ("dp", "mlp"), scatter_dimension=0, tiled=True),
    )
    up_weight_grad, down_weight_grad = (
        lax.psum_scatter(grad_up, "dp", scatter_dimension=0, tiled=True),
        lax.psum_scatter(grad_down, "dp", scatter_dimension=1, tiled=True),
    )
    half_width = grad_up_shift.shape[0]
    placed_shift = lax.dynamic_update_slice_in_dim(
        jnp.zeros((half_width * mlp_size,), jnp.float32),
        grad_up_shift,
        lax.axis_index("mlp") * half_width,
        0,
    )
    summed = lax.psum(
        (
            grad_prompts,
            grad_gain_one,
            grad_shift_one,
            grad_query_shift,
            grad_value_shift,
            grad_out_shift,
            grad_gain_two,
            grad_shift_two,
            placed_shift,
            grad_down_shift,
        ),
        ("dp", "mlp"),
    )
    up_bias_grad = lax.dynamic_slice_in_dim(
        summed[8], lax.axis_index("mlp") * half_width, half_width, 0
    )
    output = jnp.stack(outputs, axis=0)
    input_grad = jnp.stack(input_grads, axis=0)
    return (
        output,
        input_grad,
        summed[0],
        summed[1],
        summed[2],
        qkv_weight_grad,
        summed[3],
        summed[4],
        out_weight_grad,
        summed[5],
        summed[6],
        summed[7],
        up_weight_grad,
        up_bias_grad,
        down_weight_grad,
        summed[9],
    )


def solution(mesh):
    in_specs = (
        P(None, ("dp", "mlp"), None),
        P(None, ("dp", "mlp"), None),
        P(None, ("dp", "mlp"), None),
        P(None, ("dp", "mlp")),
        P(),
        P(),
        P(),
        P(),
        P(("dp", "mlp"), None),
        P(),
        P(),
        P(("dp", "mlp"), None),
        P(),
        P(),
        P(),
        P("dp", "mlp"),
        P("mlp"),
        P("mlp", "dp"),
        P(),
    )
    out_specs = (
        P(None, ("dp", "mlp"), None),
        P(None, ("dp", "mlp"), None),
        P(),
        P(),
        P(),
        P(("dp", "mlp"), None),
        P(),
        P(),
        P(("dp", "mlp"), None),
        P(),
        P(),
        P(),
        P("dp", "mlp"),
        P("mlp"),
        P("mlp", "dp"),
        P(),
    )
    return jax.shard_map(
        per_device, mesh=mesh, in_specs=in_specs, out_specs=out_specs, check_vma=False
    )
```

profile of v0, /device:TPU:0, one launch (start us, length us, event | category | flops | bytes accessed | tf_op | source)
XLA Modules:
  0.0 1096.3 jit_solution(434984600841542053)
XLA Ops:
  41.7 32.2 %all-gather.9.cloned.1.call-done = bf16[768,2304]{1,0:T(8,128)(2,1)} async-done(((bf16[24,2304]{1,0:T(8,128)(2,1)}), bf16[768,2304]{1,0:T(8,128)(2,1)}) %all-gather.9.cloned.1.call-update) | async-done | bytes 3538960 | tf_op jit(solution)/shard_map/all_gather | solution.py:154
  84.2 9.8 fusion.116
  94.0 9.2 fusion.1
  103.3 21.0 %fusion.60 = bf16[12,64,640]{2,1,0:T(8,128)(2,1)} fusion(bf16[640,12,64]{0,2,1:T(8,128)(2,1)S(1)} %bitcast.160, f32[12,640,640]{1,2,0:T(8,128)} %get-tuple-element.176, f32[12,640]{1,0:T(8,128)S(1)} %fusion.1, f32[12,640]{1,0:T(8,128)S(1)} %get-tuple-element.175), kind=kOutput, calls=%fused_computation.154 | convolution fusion | flops 644382720 | bytes 21688320 | tf_op jit(solution)/shard_map/while/body/eval_jaxpr/hqk,khd->qhd/dot_general | solution.py:88
  143.2 11.0 fusion.114
  154.1 9.6 fusion
  164.1 8.8 fusion.61
  179.8 27.7 %all-gather.13.cloned.1.call-done = bf16[1280,768]{1,0:T(8,128)(2,1)} async-done(((bf16[640,768]{1,0:T(8,128)(2,1)}), bf16[1280,768]{1,0:T(8,128)(2,1)}) %all-gather.13.cloned.1.call-update) | async-done | bytes 1966096 | tf_op jit(solution)/shard_map/all_gather | solution.py:222
  207.4 22.8 %fusion.14 = (bf16[1280,1536]{1,0:T(8,128)(2,1)}, f32[1280,1536]{1,0:T(8,128)}) fusion(f32[1536]{0:T(1024)S(1)} %convert_element_type.254, bf16[1280,768]{1,0:T(8,128)(2,1)} %all-gather.13.cloned.1.call-done, bf16[768,1536]{1,0:T(8,128)(2,1)} %all-gather.15.cloned.1.call-done), kind=kOutput, calls=%fused_computation.36 | convolution fusion | flops 3149660160 | bytes 16128000 | tf_op jit(solution)/shard_map/dot_general | solution.py:223
  230.2 10.2 all-gather.21.cloned.1.call-done
  240.5 44.4 %all-gather.17.cloned.1.call-done = bf16[1536,768]{0,1:T(8,128)(2,1)} async-done(((bf16[1536,48]{0,1:T(8,128)(2,1)}), bf16[1536,768]{0,1:T(8,128)(2,1)}) %all-gather.17.cloned.1.call-update) | async-done | bytes 2359312 | tf_op jit(solution)/shard_map/all_gather | solution.py:159
  284.9 9.0 convert_reduce_fusion.1
  307.8 21.7 %reduce-scatter.13.cloned.1.call-done = bf16[640,768]{1,0:T(8,128)(2,1)} async-done(((bf16[1280,768]{1,0:T(8,128)(2,1)}), bf16[640,768]{1,0:T(8,128)(2,1)}) %reduce-scatter.13.cloned.1.call-update) | async-done | bytes 983056 | tf_op jit(solution)/shard_map/reduce_scatter | solution.py:246
  333.7 28.6 %reduce-scatter.9.cloned.1.call-done = bf16[640,768]{1,0:T(8,128)(2,1)} async-done(((bf16[1280,768]{1,0:T(8,128)(2,1)}), bf16[640,768]{1,0:T(8,128)(2,1)}) %reduce-scatter.9.cloned.1.call-update) | async-done | bytes 983056 | tf_op jit(solution)/shard_map/reduce_scatter | solution.py:225
  367.2 28.4 %all-gather.19.cloned.1.call-done = bf16[1280,768]{1,0:T(8,128)(2,1)} async-done(((bf16[640,768]{1,0:T(8,128)(2,1)}), bf16[1280,768]{1,0:T(8,128)(2,1)}) %all-gather.19.cloned.1.call-update) | async-done | bytes 1966096 | tf_op jit(solution)/shard_map/all_gather | solution.py:222
  395.5 22.5 %fusion.17 = (bf16[1280,1536]{1,0:T(8,128)(2,1)}, f32[1280,1536]{1,0:T(8,128)}) fusion(f32[1536]{0:T(1024)S(1)} %convert_element_type.254, bf16[1280,768]{1,0:T(8,128)(2,1)} %all-gather.19.cloned.1.call-done, bf16[768,1536]{1,0:T(8,128)(2,1)} %all-gather.15.cloned.1.call-done), kind=kOutput, calls=%fused_computation.39 | convolution fusion | flops 3149660160 | bytes 16128000 | tf_op jit(solution)/shard_map/dot_general | solution.py:223
  418.0 10.6 all-gather.23.cloned.1.call-done
  428.6 9.0 convert_reduce_fusion
  451.7 8.4 fusion.119
  464.0 12.8 %multiply_reduce_fusion.1 = (f32[12,640]{1,0:T(8,128)S(1)}, f32[12,640,640]{1,2,0:T(8,128)}) fusion(f32[12,640,640]{1,2,0:T(8,128)} %get-tuple-element.172, f32[12,640]{1,0:T(8,128)S(1)} %log_add_fusion.1, bf16[640,12,64]{0,2,1:T(8,128)(2,1)S(1)} %bitcast.153, bf16[640,12,64]{0,2,1:T(8,128)(2,1)} %bitcast.162), kind=kOutput, calls=%fused_computation.8 | convolution fusion | flops 643883520 | bytes 41349120 | tf_op jit(solution)/shard_map/while/body/eval_jaxpr/qhd,khd->hqk/dot_general | solution.py:101
  476.8 14.2 %multiply_convert_fusion.1 = bf16[12,640,640]{1,2,0:T(8,128)(2,1)S(1)} fusion(f32[12,640,640]{1,2,0:T(8,128)} %get-tuple-element.184, f32[12,640,640]{1,2,0:T(8,128)} %get-tuple-element.172, f32[12,640]{1,0:T(8,128)S(1)} %get-tuple-element.183, f32[12,640]{1,0:T(8,128)S(1)} %log_add_fusion.1), kind=kLoop, calls=%fused_computation.7 | loop fusion | flops 19660800 | bytes 49213440 | tf_op jit(solution)/shard_map/while/body/eval_jaxpr/convert_element_type | solution.py:105
  498.0 11.1 %fusion.62 = bf16[12,64,640]{2,1,0:T(8,128)(2,1)} fusion(bf16[640,12,64]{0,2,1:T(8,128)(2,1)S(1)} %bitcast.154, f32[12,640,640]{1,2,0:T(8,128)} %get-tuple-element.172, f32[12,640]{1,0:T(8,128)S(1)} %log_add_fusion.1), kind=kOutput, calls=%fused_computation.156 | convolution fusion | flops 639467520 | bytes 21657600 | tf_op jit(solution)/shard_map/while/body/eval_jaxpr/hqk,qhd->khd/dot_general | solution.py:112
  518.6 12.3 %multiply_reduce_fusion = (f32[12,640]{1,0:T(8,128)S(1)}, f32[12,640,640]{1,2,0:T(8,128)}) fusion(f32[12,640,640]{1,2,0:T(8,128)} %get-tuple-element.176, f32[12,640]{1,0:T(8,128)S(1)} %log_add_fusion, bf16[640,12,64]{0,2,1:T(8,128)(2,1)S(1)} %bitcast.155, bf16[640,12,64]{0,2,1:T(8,128)(2,1)S(1)} %bitcast.161), kind=kOutput, calls=%fused_computation.5 | convolution fusion | flops 643883520 | bytes 41349120 | tf_op jit(solution)/shard_map/while/body/eval_jaxpr/qhd,khd->hqk/dot_general | solution.py:101
  530.9 13.5 %multiply_convert_fusion = bf16[12,640,640]{1,2,0:T(8,128)(2,1)S(1)} fusion(f32[12,640,640]{1,2,0:T(8,128)} %get-tuple-element.186, f32[12,640,640]{1,2,0:T(8,128)} %get-tuple-element.176, f32[12,640]{1,0:T(8,128)S(1)} %get-tuple-element.185, f32[12,640]{1,0:T(8,128)S(1)} %log_add_fusion), kind=kLoop, calls=%fused_computation.4 | loop fusion | flops 19660800 | bytes 49213440 | tf_op jit(solution)/shard_map/while/body/eval_jaxpr/convert_element_type | solution.py:105
  549.4 10.3 fusion.65
  575.5 9.6 convolution_add_fusion.3
  619.9 40.8 %all-reduce = (f32[768]{0:T(1024)}, f32[768]{0:T(1024)}, f32[768]{0:T(1024)}, f32[768]{0:T(1024)}, f32[768]{0:T(1024)}, /*index=5*/f32[768]{0:T(1024)}, f32[768]{0:T(1024)}, f32[3072]{0:T(1024)S(1)}, f32[768]{0:T(1024)}) all-reduce(f32[768]{0:T(1024)S(1)} %add.401, ...), channel_id=1, replica_groups=mesh['dp'=16,'mlp'=2] {'dp','mlp'}, use_global_device_ids=true, to_apply=%region_35.38 | all-reduce | flops 9216 | bytes 73728 | tf_op jit(solution)/shard_map/psum | solution.py:313
  668.9 28.6 %all-reduce.3.cloned.1.call-done = f32[50,768]{1,0:T(8,128)} async-done(((f32[50,768]{1,0:T(8,128)}), f32[50,768]{1,0:T(8,128)}) %all-reduce.3.cloned.1.call-update) | async-done | bytes 153616 | tf_op jit(solution)/shard_map/psum | solution.py:313
  697.6 81.9 %reduce-scatter.23.cloned.1.call-done = f32[1536,48]{0,1:T(8,128)} async-done(((f32[1536,768]{0,1:T(8,128)}), f32[1536,48]{0,1:T(8,128)}) %reduce-scatter.23.cloned.1.call-update) | async-done | bytes 294928 | tf_op jit(solution)/shard_map/reduce_scatter | solution.py:304
  779.5 79.4 %reduce-scatter.21.cloned.1.call-done = f32[48,1536]{1,0:T(8,128)} async-done(((f32[768,1536]{1,0:T(8,128)}), f32[48,1536]{1,0:T(8,128)}) %reduce-scatter.21.cloned.1.call-update) | async-done | bytes 294928 | tf_op jit(solution)/shard_map/reduce_scatter | solution.py:303
  858.9 103.8 %reduce-scatter.19.cloned.1.call-done = f32[24,768]{1,0:T(8,128)} async-done(((f32[768,768]{1,0:T(8,128)}), f32[24,768]{1,0:T(8,128)}) %reduce-scatter.19.cloned.1.call-update) | async-done | bytes 73744 | tf_op jit(solution)/shard_map/reduce_scatter | solution.py:300
  962.7 125.3 %reduce-scatter.17.cloned.1.call-done = f32[24,2304]{1,0:T(8,128)} async-done(((f32[768,2304]{1,0:T(8,128)}), f32[24,2304]{1,0:T(8,128)}) %reduce-scatter.17.cloned.1.call-update) | async-done | bytes 221200 | tf_op jit(solution)/shard_map/reduce_scatter | solution.py:299
  (385 shorter events, 189.3 us)
Async XLA Ops:
  7.2 66.7 %all-gather.9.cloned.1.call-start = ((), (), s32[]{:S(2)}) async-start(), calls=%async_computation.8 | async-start | bytes 3649536 | tf_op jit(solution)/shard_map/all_gather | solution.py:154
  7.9 121.8 %all-gather.11.cloned.1.call-start = ((), (), s32[]{:S(2)}) async-start(), calls=%async_computation.9 | async-start | bytes 1216512 | tf_op jit(solution)/shard_map/all_gather | solution.py:155
  8.7 171.1 %all-gather.15.cloned.1.call-start = ((), (), s32[]{:S(2)}) async-start(), calls=%async_computation.11 | async-start | bytes 2506752 | tf_op jit(solution)/shard_map/all_gather | solution.py:158
  9.4 198.0 %all-gather.13.cloned.1.call-start = ((), (), s32[]{:S(2)}) async-start(), calls=%async_computation.10 | async-start | bytes 2949120 | tf_op jit(solution)/shard_map/all_gather | solution.py:222
  39.4 39.1 %copy-start.4 = (f32[640,768]{1,0:T(8,128)}, f32[640,768]{1,0:T(8,128)S(1)}, u32[]{:S(2)}) copy-start(f32[640,768]{1,0:T(8,128)S(1)} %get-tuple-element.141) | copy-start | bytes 5898244
  39.4 39.1 %copy-start.59 = (f32[640]{0:T(1024)}, f32[640]{0:T(1024)S(1)}, u32[]{:S(2)}) copy-start(f32[640]{0:T(1024)S(1)} %broadcast_multiply_fusion.1) | copy-start | bytes 7684
  39.8 38.7 %copy-start.71 = (f32[640]{0:T(1024)}, f32[640]{0:T(1024)S(1)}, u32[]{:S(2)}) copy-start(f32[640]{0:T(1024)S(1)} %multiply_reduce_fusion.7) | copy-start | bytes 7684
  39.8 38.7 %copy-start.63 = (f32[640]{0:T(1024)}, f32[640]{0:T(1024)S(1)}, u32[]{:S(2)}) copy-start(f32[640]{0:T(1024)S(1)} %fusion.86) | copy-start | bytes 7684
  39.8 93.3 %copy-start.51 = (f32[768]{0:T(1024)}, f32[768]{0:T(1024)S(1)}, u32[]{:S(2)}) copy-start(f32[768]{0:T(1024)S(1)} %convert_element_type.240) | copy-start | bytes 9220
  39.9 93.3 %copy-start.53 = (f32[768]{0:T(1024)}, f32[768]{0:T(1024)S(1)}, u32[]{:S(2)}) copy-start(f32[768]{0:T(1024)S(1)} %convert_element_type.241) | copy-start | bytes 9220
  39.9 93.2 %copy-start.68 = (f32[640]{0:T(1024)}, f32[640]{0:T(1024)S(1)}, u32[]{:S(2)}) copy-start(f32[640]{0:T(1024)S(1)} %broadcast_multiply_fusion.3) | copy-start | bytes 7684
  41.6 91.6 %copy-start.84 = (f32[640]{0:T(1024)}, f32[640]{0:T(1024)S(1)}, u32[]{:S(2)}) copy-start(f32[640]{0:T(1024)S(1)} %fusion.84) | copy-start | bytes 7684
  103.2 21.0 %copy-start.55 = (f32[12,640]{1,0:T(8,128)}, f32[12,640]{1,0:T(8,128)S(1)}, u32[]{:S(2)}) copy-start(f32[12,640]{1,0:T(8,128)S(1)} %fusion.1) | copy-start | bytes 92164
  133.1 41.4 %copy-start = (f32[640,768]{1,0:T(8,128)}, f32[640,768]{1,0:T(8,128)S(1)}, u32[]{:S(2)}) copy-start(f32[640,768]{1,0:T(8,128)S(1)} %get-tuple-element.178) | copy-start | bytes 5898244
  133.6 41.0 %copy-start.61 = (f32[640]{0:T(1024)}, f32[640]{0:T(1024)S(1)}, u32[]{:S(2)}) copy-start(f32[640]{0:T(1024)S(1)} %broadcast_multiply_fusion) | copy-start | bytes 7684
  176.6 63.9 %all-gather.21.cloned.1.call-start = ((), (), s32[]{:S(2)}) async-start(), calls=%async_computation.16 | async-start | bytes 2949120 | tf_op jit(solution)/shard_map/all_gather | solution.py:237
  179.1 105.8 %all-gather.17.cloned.1.call-start = ((), (), s32[]{:S(2)}) async-start(), calls=%async_computation.12 | async-start | bytes 2506752 | tf_op jit(solution)/shard_map/all_gather | solution.py:159
  179.7 149.9 %reduce-scatter.13.cloned.1.call-start = ((), (), s32[]{:S(2)}) async-start(), calls=%async_computation.17 | async-start | bytes 2949120 | tf_op jit(solution)/shard_map/reduce_scatter | solution.py:246
  300.2 62.1 %reduce-scatter.9.cloned.1.call-start = ((), (), s32[]{:S(2)}) async-start(), calls=%async_computation.13 | async-start | bytes 2949120 | tf_op jit(solution)/shard_map/reduce_scatter | solution.py:225
  307.0 22.6 %copy-start.3 = (f32[640,768]{1,0:T(8,128)S(1)}, f32[640,768]{1,0:T(8,128)}, u32[]{:S(2)}) copy-start(f32[640,768]{1,0:T(8,128)} %copy-done.2) | copy-start | bytes 5898244
  307.0 88.5 %all-gather.19.cloned.1.call-start = ((), (), s32[]{:S(2)}) async-start(), calls=%async_computation.14 | async-start | bytes 2949120 | tf_op jit(solution)/shard_map/all_gather | solution.py:222
  307.8 120.9 %all-gather.23.cloned.1.call-start = ((), (), s32[]{:S(2)}) async-start(), calls=%async_computation.18 | async-start | bytes 2949120 | tf_op jit(solution)/shard_map/all_gather | solution.py:237
  307.8 54.5 %copy-start.70 = (f32[640]{0:T(1024)S(1)}, f32[640]{0:T(1024)}, u32[]{:S(2)}) copy-start(f32[640]{0:T(1024)} %get-tuple-element.194) | copy-start | bytes 7684
  367.1 142.0 %reduce-scatter.15.cloned.1.call-start = ((), (), s32[]{:S(2)}) async-start(), calls=%async_computation.19 | async-start | bytes 2949120 | tf_op jit(solution)/shard_map/reduce_scatter | solution.py:246
  444.0 68.2 %reduce-scatter.11.cloned.1.call-start = ((), (), s32[]{:S(2)}) async-start(), calls=%async_computation.15 | async-start | bytes 2949120 | tf_op jit(solution)/shard_map/reduce_scatter | solution.py:225
  451.6 245.9 %all-reduce.3.cloned.1.call-start = ((), (), s32[]{:S(2)}) async-start(), calls=%async_computation.20 | async-start | bytes 344064 | tf_op jit(solution)/shard_map/psum | solution.py:313
  575.4 204.0 %reduce-scatter.23.cloned.1.call-start = ((), (), s32[]{:S(2)}) async-start(), calls=%async_computation.24 | async-start | bytes 5013504 | tf_op jit(solution)/shard_map/reduce_scatter | solution.py:304
  585.1 273.8 %reduce-scatter.21.cloned.1.call-start = ((), (), s32[]{:S(2)}) async-start(), calls=%async_computation.23 | async-start | bytes 5013504 | tf_op jit(solution)/shard_map/reduce_scatter | solution.py:303
  596.3 366.3 %reduce-scatter.19.cloned.1.call-start = ((), (), s32[]{:S(2)}) async-start(), calls=%async_computation.22 | async-start | bytes 2433024 | tf_op jit(solution)/shard_map/reduce_scatter | solution.py:300
  602.3 485.7 %reduce-scatter.17.cloned.1.call-start = ((), (), s32[]{:S(2)}) async-start(), calls=%async_computation.21 | async-start | bytes 7299072 | tf_op jit(solution)/shard_map/reduce_scatter | solution.py:299
  617.8 46.5 %copy-start.8 = (f32[640,768]{1,0:T(8,128)S(1)}, f32[640,768]{1,0:T(8,128)}, u32[]{:S(2)}) copy-start(f32[640,768]{1,0:T(8,128)} %get-tuple-element.136) | copy-start | bytes 5898244
  617.8 46.5 %copy-start.93 = (pred[640]{0:T(1024)(128)(4,1)S(1)}, pred[640]{0:T(1024)(128)(4,1)}, u32[]{:S(2)}) copy-start(pred[640]{0:T(1024)(128)(4,1)} %copy-done.92) | copy-start | bytes 1924
  (99 other events, 534.2 us)
Sparse Core Ops, SparseCore 0:
  10.9 62.8 all-gather.8
  76.8 52.9 all-gather.10
  132.0 41.1 all-gather.14
  176.7 30.6 all-gather.12
  208.8 31.6 all-gather.20
  242.6 42.2 all-gather.16
  300.3 29.1 reduce-scatter.12
  331.9 30.3 reduce-scatter.8
  363.9 31.6 all-gather.18
  396.9 31.6 all-gather.22
  444.1 30.3 reduce-scatter.14
  476.8 30.3 reduce-scatter.10
  575.6 121.9 all-reduce.2
  701.8 77.5 reduce-scatter.22
  784.2 74.5 reduce-scatter.20
  864.6 98.0 reduce-scatter.18
  969.7 118.1 reduce-scatter.16
where the time goes:
time: 1110 us; the launch traced here: 1100 us
  waiting for transfers between devices  632 us (57%)
  matrix products  268 us (24%)
  other arithmetic  91.8 us (8%)
  local copies, waits for them, and re-layouts  44.5 us (4%)
  blocking collectives  40.8 us (4%)
  between operations  18.5 us (2%)
    reduce_scatter x1, waiting for transfers between devices, per_device(): lax.psum_scatter(grad_qkv, ('dp', 'mlp'), scatter_dimension=0, tiled=True)  125 us
    reduce_scatter x1, waiting for transfers between devices, per_device(): lax.psum_scatter(grad_out, ('dp', 'mlp'), scatter_dimension=0, tiled=True)  104 us
    reduce_scatter x1, waiting for transfers between devices, per_device(): lax.psum_scatter(grad_down, 'dp', scatter_dimension=1, tiled=True)  81.9 us
    reduce_scatter x1, waiting for transfers between devices, per_device(): lax.psum_scatter(grad_up, 'dp', scatter_dimension=0, tiled=True)  79.4 us
    all_gather x2, waiting for transfers between devices, per_device(): gathered_piece = lax.all_gather(normed_two, 'mlp', axis=0, tiled=True)  56 us
    dot_general x2, matrix products, per_device(): jnp.dot(gathered_piece, up_use, preferred_element_type=jnp.float32)  45.3 us
    all_gather x1, waiting for transfers between devices, per_device(): lax.all_gather(down_weight, 'dp', axis=1, tiled=True)  44.4 us
    psum x1, blocking collectives, per_device(): lax.psum((grad_prompts, grad_gain_one, grad_shift_one, grad_query_shift,...  40.8 us
  transfers between devices with their start and end apart: 17, of which 14 were waited for; matrix products, arithmetic and copies ran while one was open for 28% of the time, Pallas kernels for 0%

commit v1 on v0

v1 whole, which is shorter than its diff:
```python
import math

import jax
import jax.numpy as jnp
from jax import lax
from jax.experimental import pallas as pl
from jax.experimental.pallas import tpu as pltpu
from jax.sharding import PartitionSpec as P

D = 768
HEADS = 12
HEAD_DIM = 64
PAIRS = 6
PROMPTS = 50
LEN_LOW = 101
LEN_MID = 197
TABLE = 875
SLOTS = 4
ROWS = 640
GROUP = 3 * 128

epsilon = 1e-06
highest = lax.Precision.HIGHEST
bf16 = jnp.bfloat16
f32 = jnp.float32
log2_e = 1.4426950408889634
score_scale = log2_e / math.sqrt(HEAD_DIM)
erf_p = 0.3275911
erf_a = (0.254829592, -0.284496736, 1.421413741, -1.453152027, 1.061405429)

NT = (((1,), (1,)), ((), ()))
NN = (((1,), (0,)), ((), ()))
TN = (((0,), (0,)), ((), ()))


def dot(left, right, dims=NN):
    return lax.dot_general(left, right, dims, preferred_element_type=f32)


def layout(slot_lengths, bucket_id):
    sizes_used = jnp.where(slot_lengths > 0, slot_lengths + PROMPTS, 0)
    seq_ends = jnp.cumsum(sizes_used)
    seq_starts = seq_ends - sizes_used
    row_ids = jnp.arange(ROWS, dtype=jnp.int32)
    sequence = jnp.sum((seq_ends[None, :] <= row_ids[:, None]).astype(jnp.int32), axis=1)
    slot_ids = jnp.arange(SLOTS, dtype=jnp.int32)
    own_start = jnp.sum(
        jnp.where(sequence[:, None] == slot_ids[None, :], seq_starts[None, :], 0), axis=1
    )
    position = row_ids - own_start
    inside = sequence < SLOTS
    is_prompt = inside & (position < PROMPTS)
    is_image = inside & (position >= PROMPTS)
    table_start = jnp.where(
        bucket_id == 0, 0, jnp.where(bucket_id == 1, LEN_LOW, LEN_LOW + LEN_MID)
    ).astype(jnp.int32)
    table_index = jnp.clip(table_start + position - PROMPTS, 0, TABLE - 1)
    prompt_index = jnp.clip(position, 0, PROMPTS - 1)
    return (sequence, inside, is_prompt, is_image, table_index, prompt_index)


def norm_stats(values_in):
    average = jnp.mean(values_in, axis=-1, keepdims=True)
    centred = values_in - average
    variance = jnp.mean(centred * centred, axis=-1, keepdims=True)
    inverse = lax.rsqrt(variance + epsilon)
    return centred * inverse, inverse


def norm_back(grad_normed, normal, inverse, gain):
    scaled = grad_normed * gain
    mean_one = jnp.mean(scaled, axis=-1, keepdims=True)
    mean_two = jnp.mean(scaled * normal, axis=-1, keepdims=True)
    return (scaled - mean_one - normal * mean_two) * inverse


def attend_kernel(qkv_ref, fq_ref, fk_ref, o_ref, lse_ref, *, chunk):
    pair = pl.program_id(1)
    lane = lax.broadcasted_iota(jnp.int32, (1, 128), 1)
    keys = jnp.concatenate([qkv_ref[:, 128:256], fk_ref[...]], axis=1)
    values = jnp.concatenate([qkv_ref[:, 256:384], jnp.ones((ROWS, 128), bf16)], axis=1)
    for step in range(ROWS // chunk):
        rows = slice(step * chunk, (step + 1) * chunk)
        queries = qkv_ref[rows, 0:128]
        marks = fq_ref[rows, :]
        outs = []
        lse = lse_ref[rows, :]
        for half in range(2):
            keep = (lane < 64) if half == 0 else (lane >= 64)
            own = jnp.concatenate([jnp.where(keep, queries, jnp.zeros_like(queries)), marks], axis=1)
            scores = dot(own, keys, NT)
            top = jnp.max(scores, axis=1, keepdims=True)
            weights = jnp.exp2((scores - top) * score_scale)
            mixed = dot(weights.astype(bf16), values)
            total = mixed[:, 128:129]
            outs.append(mixed[:, :128] / total)
            log_total = top + jnp.log2(total) * (1.0 / score_scale)
            lse = jnp.where(lane == pair * 2 + half, log_total, lse)
        o_ref[rows, :] = jnp.where(lane < 64, outs[0], outs[1]).astype(bf16)
        lse_ref[rows, :] = lse


def attend(qkv, fq, fk, chunk=320):
    rows = qkv.shape[0]
    mark = pl.BlockSpec((ROWS, 128), lambda b, p: (b, 0))
    return pl.pallas_call(
        lambda *refs: attend_kernel(*refs, chunk=chunk),
        grid=(rows // ROWS, PAIRS),
        in_specs=[pl.BlockSpec((ROWS, GROUP), lambda b, p: (b, p)), mark, mark],
        out_specs=[pl.BlockSpec((ROWS, 128), lambda b, p: (b, p)), mark],
        out_shape=[
            jax.ShapeDtypeStruct((rows, D), bf16),
            jax.ShapeDtypeStruct((rows, 128), f32),
        ],
        compiler_params=pltpu.CompilerParams(
            dimension_semantics=("arbitrary", "arbitrary"), vmem_limit_bytes=40 << 20
        ),
        cost_estimate=pl.CostEstimate(
            flops=16 * rows * ROWS * D, bytes_accessed=rows * D * 8, transcendentals=rows * ROWS * HEADS
        ),
        name="attend",
    )(qkv, fq, fk)


def split_three(value):
    first = value.astype(bf16)
    rest = value - first.astype(f32)
    second = rest.astype(bf16)
    third = (rest - second.astype(f32)).astype(bf16)
    return first, second, third


def attend_back_kernel(qkv_ref, do_ref, o_ref, fq_ref, fk_ref, lse_ref, dqkv_ref, ds_ref, *, chunk):
    pair = pl.program_id(1)
    lane = lax.broadcasted_iota(jnp.int32, (1, 128), 1)
    queries = qkv_ref[:, 0:128]
    grads = do_ref[...]
    marks = fq_ref[...]
    product = grads.astype(f32) * o_ref[...].astype(f32)
    lse = lse_ref[...]
    zero = jnp.zeros_like(queries)
    own_q, own_g, wide_q, wide_g = [], [], [], []
    for half in range(2):
        keep = (lane < 64) if half == 0 else (lane >= 64)
        shift = -jnp.sum(jnp.where(lane == pair * 2 + half, lse, 0.0), axis=1, keepdims=True)
        inner = -jnp.sum(jnp.where(keep, product, 0.0), axis=1, keepdims=True)
        s0, s1, s2 = split_three(shift)
        i0, i1, i2 = split_three(inner)
        mark_q = jnp.where(lane == 8, s0, jnp.where(lane == 9, s1, jnp.where(lane == 10, s2, marks)))
        mark_g = jnp.where(lane == 8, i0, jnp.where(lane == 9, i1, jnp.where(lane == 10, i2, zero)))
        q_half = jnp.where(keep, queries, zero)
        g_half = jnp.where(keep, grads, zero)
        own_q.append(q_half)
        own_g.append(g_half)
        wide_q.append(jnp.concatenate([q_half, mark_q], axis=1))
        wide_g.append(jnp.concatenate([g_half, mark_g], axis=1))
    for step in range(ROWS // chunk):
        rows = slice(step * chunk, (step + 1) * chunk)
        keys = jnp.concatenate([qkv_ref[rows, 128:256], fk_ref[rows, :]], axis=1)
        values = jnp.concatenate([qkv_ref[rows, 256:384], fk_ref[rows, :]], axis=1)
        dv = jnp.zeros((chunk, 128), f32)
        dk = jnp.zeros((chunk, 128), f32)
        for half in range(2):
            weights = jnp.exp2(dot(keys, wide_q[half], NT) * score_scale)
            ds = (weights * dot(values, wide_g[half], NT)).astype(bf16)
            ds_ref[half, rows, :] = ds
            dv = dv + dot(weights.astype(bf16), own_g[half])
            dk = dk + dot(ds, own_q[half])
        dqkv_ref[rows, 256:384] = dv.astype(bf16)
        dqkv_ref[rows, 128:256] = (dk * 0.125).astype(bf16)
    keys_t = qkv_ref[:, 128:256].T
    dq = [dot(keys_t, ds_ref[half]).T for half in range(2)]
    dqkv_ref[:, 0:128] = (jnp.where(lane < 64, dq[0], dq[1]) * 0.125).astype(bf16)


def attend_back(qkv, do, o, fq, fk, lse, chunk=640):
    rows = qkv.shape[0]
    mark = pl.BlockSpec((ROWS, 128), lambda b, p: (b, 0))
    part = pl.BlockSpec((ROWS, 128), lambda b, p: (b, p))
    group = pl.BlockSpec((ROWS, GROUP), lambda b, p: (b, p))
    return pl.pallas_call(
        lambda *refs: attend_back_kernel(*refs, chunk=chunk),
        grid=(rows // ROWS, PAIRS),
        in_specs=[group, part, part, mark, mark, mark],
        out_specs=group,
        out_shape=jax.ShapeDtypeStruct(qkv.shape, bf16),
        scratch_shapes=[pltpu.VMEM((2, ROWS, ROWS), bf16)],
        compiler_params=pltpu.CompilerParams(
            dimension_semantics=("arbitrary", "arbitrary"), vmem_limit_bytes=40 << 20
        ),
        cost_estimate=pl.CostEstimate(
            flops=40 * rows * ROWS * D, bytes_accessed=rows * D * 16, transcendentals=rows * ROWS * HEADS
        ),
        name="attend_back",
    )(qkv, do, o, fq, fk, lse)


def gelu_parts(u):
    z = jnp.abs(u) * 0.7071067811865476
    t = 1.0 / (1.0 + erf_p * z)
    e = jnp.exp2(u * u * (-0.5 * log2_e))
    series = t * (erf_a[0] + t * (erf_a[1] + t * (erf_a[2] + t * (erf_a[3] + t * erf_a[4]))))
    tail = 0.5 * series * e
    return jnp.where(u < 0, tail, 1.0 - tail), e * 0.3989422804014327


def feed_kernel(
    b_ref, gm_ref, up_ref, dn_ref, ub_ref, h_ref, db_ref, gu_ref, gd_ref, gub_ref,
    act_s, du_s, h_s, db_s, *, chunk, steps,
):
    j = pl.program_id(0)
    rows_all = b_ref.shape[0]
    up, dn, ub = up_ref[...], dn_ref[...], ub_ref[...]
    sums = jnp.zeros((1, ub.shape[1]), f32)
    for step in range(rows_all // chunk):
        rows = slice(step * chunk, (step + 1) * chunk)
        u = dot(b_ref[rows, :], up) + ub
        cdf, pdf = gelu_parts(u)
        act = (u * cdf).astype(bf16)
        du = (dot(gm_ref[rows, :], dn) * (cdf + u * pdf)).astype(bf16)
        sums = sums + jnp.sum(du.astype(f32), axis=0, keepdims=True)
        act_s[rows, :] = act
        du_s[rows, :] = du
        hh = dot(act, dn, NT)
        dd = dot(du, up, NT)

        @pl.when(j == 0)
        def _():
            h_s[rows, :] = hh
            db_s[rows, :] = dd

        @pl.when(j > 0)
        def _():
            h_s[rows, :] += hh
            db_s[rows, :] += dd

    gub_ref[...] = sums
    gu_ref[...] = dot(b_ref[...], du_s[...], TN).astype(bf16)
    gd_ref[...] = dot(gm_ref[...], act_s[...], TN).astype(bf16)

    @pl.when(j == steps - 1)
    def _():
        h_ref[...] = h_s[...]
        db_ref[...] = db_s[...]


def feed(b, gm, up, dn, ub, block=512, chunk=640):
    rows = b.shape[0]
    splits, _, hidden = up.shape
    per = hidden // block
    steps = splits * per
    full = pl.BlockSpec((rows, D), lambda j: (0, 0), pipeline_mode=pl.Buffered(1))
    weight = pl.BlockSpec((None, D, block), lambda j: (j // per, 0, j % per))
    bias = pl.BlockSpec((1, block), lambda j: (0, j))
    return pl.pallas_call(
        lambda *refs: feed_kernel(*refs, chunk=chunk, steps=steps),
        grid=(steps,),
        in_specs=[full, full, weight, weight, bias],
        out_specs=[full, full, weight, weight, bias],
        out_shape=[jax.ShapeDtypeStruct((rows, D), f32)] * 2
        + [jax.ShapeDtypeStruct(up.shape, bf16)] * 2
        + [jax.ShapeDtypeStruct(ub.shape, f32)],
        scratch_shapes=[pltpu.VMEM((rows, block), bf16)] * 2 + [pltpu.VMEM((rows, D), f32)] * 2,
        compiler_params=pltpu.CompilerParams(
            dimension_semantics=("arbitrary",), vmem_limit_bytes=56 << 20
        ),
        cost_estimate=pl.CostEstimate(
            flops=12 * rows * steps * block * D,
            bytes_accessed=rows * D * 12 + steps * block * D * 8,
            transcendentals=2 * rows * steps * block,
        ),
        name="feed",
    )(b, gm, up, dn, ub)


def pair_major(columns):
    lead = columns.shape[:-1]
    return columns.reshape(lead + (3, PAIRS, 128)).swapaxes(-3, -2).reshape(lead + (3 * D,))


def pair_minor(columns):
    lead = columns.shape[:-1]
    return columns.reshape(lead + (PAIRS, 3, 128)).swapaxes(-3, -2).reshape(lead + (3 * D,))


def per_device(
    tokens,
    cotangent,
    lengths,
    buckets,
    pos_table,
    prompts,
    norm1_gain,
    norm1_bias,
    qkv_weight,
    q_bias,
    v_bias,
    out_weight,
    out_bias,
    norm2_gain,
    norm2_bias,
    up_weight,
    up_bias,
    down_weight,
    down_bias,
):
    everyone = ("dp", "mlp")
    mlp_size = lax.axis_size("mlp")
    micro_count, local_rows = tokens.shape[:2]
    rows = micro_count * local_rows
    hidden_local = up_weight.shape[1]
    hidden = hidden_local * mlp_size

    qkv_full = lax.all_gather(pair_major(qkv_weight), everyone, axis=0, tiled=True)
    out_full = lax.all_gather(out_weight, everyone, axis=0, tiled=True)
    up_full = lax.all_gather(up_weight, ("mlp", "dp"), axis=0, tiled=True)
    down_full = lax.all_gather(down_weight.T, ("mlp", "dp"), axis=0, tiled=True)
    up_full = up_full.reshape(mlp_size, D, hidden_local)
    down_full = down_full.reshape(mlp_size, D, hidden_local)
    up_shift = lax.all_gather(up_bias, "mlp", axis=0, tiled=True).astype(f32)[None, :]

    gain_one, shift_one = norm1_gain.astype(f32), norm1_bias.astype(f32)
    gain_two, shift_two = norm2_gain.astype(f32), norm2_bias.astype(f32)
    qkv_offset = pair_major(
        jnp.concatenate([q_bias.astype(f32), jnp.zeros((D,), f32), v_bias.astype(f32)])
    )

    flat = jax.vmap(layout)(lengths.reshape(-1, SLOTS), buckets.reshape(-1))
    sequence, inside, is_prompt, is_image, table_index, prompt_index = (
        item.reshape(rows) for item in flat
    )
    valid = inside[:, None]
    image = is_image[:, None]
    table_all = jnp.concatenate([pos_table, prompts], axis=0)
    picked = jnp.take(table_all, jnp.where(is_prompt, TABLE + prompt_index, table_index), axis=0)
    image_rows = tokens.reshape(rows, D).astype(f32)
    start_rows = jnp.where(
        valid, jnp.where(image, image_rows, 0.0) + picked.astype(f32), 0.0
    )
    lane = jnp.arange(128, dtype=jnp.int32)[None, :]
    same = lane == sequence[:, None]
    fq = same.astype(bf16)
    fk = jnp.where(
        lane <= SLOTS,
        jnp.where(same, 0.0, -1e30),
        jnp.where((lane >= 8) & (lane < 11), 1.0, 0.0),
    ).astype(bf16)
    grad_branch = jnp.where(valid, cotangent.reshape(rows, D), jnp.zeros((), bf16))
    grad_two = grad_branch.astype(f32)
    grad_down_shift = jnp.sum(grad_two, axis=0)

    normal_one, inverse_one = norm_stats(start_rows)
    normed = (normal_one * gain_one + shift_one).astype(bf16)
    qkv_rows = (dot(normed, qkv_full) + qkv_offset).astype(bf16)
    attended, log_total = attend(qkv_rows, fq, fk)
    first_sum = start_rows + dot(attended, out_full) + out_bias.astype(f32)
    normal_two, inverse_two = norm_stats(first_sum)
    normed_two = (normal_two * gain_two + shift_two).astype(bf16)

    branch, grad_normed, grad_up, grad_down, grad_up_shift = feed(
        normed_two, grad_branch, up_full, down_full, up_shift
    )
    output = jnp.where(valid, first_sum + branch + down_bias.astype(f32), 0.0).astype(bf16)

    grad_gain_two = jnp.sum(grad_normed * normal_two, axis=0)
    grad_shift_two = jnp.sum(grad_normed, axis=0)
    grad_one = grad_two + norm_back(grad_normed, normal_two, inverse_two, gain_two)
    grad_out_shift = jnp.sum(grad_one, axis=0)
    grad_att = grad_one.astype(bf16)
    grad_out = dot(attended, grad_att, TN).astype(bf16)
    grad_attended = dot(grad_att, out_full, NT).astype(bf16)
    grad_qkv_rows = attend_back(qkv_rows, grad_attended, attended, fq, fk, log_total)
    grad_qkv = dot(normed, grad_qkv_rows, TN).astype(bf16)
    column_sums = pair_minor(jnp.sum(grad_qkv_rows.astype(f32), axis=0))
    grad_normed_one = dot(grad_qkv_rows, qkv_full, NT)
    grad_gain_one = jnp.sum(grad_normed_one * normal_one, axis=0)
    grad_shift_one = jnp.sum(grad_normed_one, axis=0)
    grad_zero = grad_one + norm_back(grad_normed_one, normal_one, inverse_one, gain_one)
    input_grad = jnp.where(image, grad_zero, 0.0)
    prompt_hits = (
        (prompt_index[:, None] == jnp.arange(PROMPTS, dtype=jnp.int32)[None, :]) & is_prompt[:, None]
    ).astype(f32)
    grad_prompts = jnp.einsum("rp,rd->pd", prompt_hits, grad_zero, precision=highest)

    def scatter(value, axes):
        return lax.psum_scatter(value, axes, scatter_dimension=0, tiled=True).astype(f32)

    qkv_weight_grad = pair_minor(scatter(grad_qkv, everyone))
    out_weight_grad = scatter(grad_out, everyone)
    up_weight_grad = scatter(grad_up.reshape(mlp_size * D, hidden_local), ("mlp", "dp"))
    down_weight_grad = scatter(grad_down.reshape(mlp_size * D, hidden_local), ("mlp", "dp")).T

    packed = jnp.concatenate(
        [
            grad_prompts,
            grad_gain_one[None],
            grad_shift_one[None],
            column_sums[None, :D],
            column_sums[None, 2 * D :],
            grad_out_shift[None],
            grad_gain_two[None],
            grad_shift_two[None],
            grad_down_shift[None],
            grad_up_shift.reshape(hidden // D, D),
        ],
        axis=0,
    )
    summed = lax.psum(packed, everyone)
    singles = [summed[PROMPTS + i] for i in range(8)]
    up_bias_grad = lax.dynamic_slice_in_dim(
        summed[PROMPTS + 8 :].reshape(hidden), lax.axis_index("mlp") * hidden_local, hidden_local, 0
    )
    return (
        output.reshape(tokens.shape),
        input_grad.reshape(tokens.shape),
        summed[:PROMPTS],
        singles[0],
        singles[1],
        qkv_weight_grad,
        singles[2],
        singles[3],
        out_weight_grad,
        singles[4],
        singles[5],
        singles[6],
        up_weight_grad,
        up_bias_grad,
        down_weight_grad,
        singles[7],
    )


def solution(mesh):
    both = ("dp", "mlp")
    in_specs = (
        P(None, both, None),
        P(None, both, None),
        P(None, both, None),
        P(None, both),
        P(),
        P(),
        P(),
        P(),
        P(both, None),
        P(),
        P(),
        P(both, None),
        P(),
        P(),
        P(),
        P("dp", "mlp"),
        P("mlp"),
        P("mlp", "dp"),
        P(),
    )
    out_specs = (
        P(None, both, None),
        P(None, both, None),
        P(),
        P(),
        P(),
        P(both, None),
        P(),
        P(),
        P(both, None),
        P(),
        P(),
        P(),
        P("dp", "mlp"),
        P("mlp"),
        P("mlp", "dp"),
        P(),
    )
    return jax.shard_map(
        per_device, mesh=mesh, in_specs=in_specs, out_specs=out_specs, check_vma=False
    )
```

time: 1110 us -> 960 us (0.86)
  matrix products: 268 us -> 39.6 us
  Pallas kernels: 0 us -> 117 us
  waiting for transfers between devices: 632 us -> 713 us
  other arithmetic: 91.8 us -> 41.6 us
  blocking collectives: 40.8 us -> 5.54 us
  local copies, waits for them, and re-layouts: 44.5 us -> 23.8 us
    dot_general x36 -> x6, matrix products: 265 us -> 37.6 us  [dot(): return lax.dot_general(left, right, dims, preferred_element_type=f32)]
    pallas_call x0 -> x3, Pallas kernels: none -> 117 us  [the longest x1 60.9 us: feed(): pl.pallas_call(lambda *refs: feed_kernel(*refs, chunk=chunk, steps=steps)...]
    psum x1, waiting for transfers between devices: 28.6 us -> 104 us  [per_device(): summed = lax.psum(packed, everyone)]
    psum x1 -> x0, blocking collectives: 40.8 us -> none  [per_device(): lax.psum((grad_prompts, grad_gain_one, grad_shift_one, grad_query_shift,...]
    reduce_sum x16 -> x6, other arithmetic: 46.9 us -> 16.8 us  [the longest x1 5.39 us: per_device(): grad_out_shift = jnp.sum(grad_one, axis=0)]
    convert_element_type x16 -> x11, other arithmetic: 34.3 us -> 5.48 us  [the longest x2 3.05 us: scatter(): lax.psum_scatter(value, axes, scatter_dimension=0, tiled=True).astype(f32)]
    all_gather x8 -> x4, waiting for transfers between devices: 159 us -> 181 us  [the longest x1 65.1 us: per_device(): down_full = lax.all_gather(down_weight.T, ('mlp', 'dp'), axis=0, tiled=True)]
    reduce_scatter x8 -> x4, waiting for transfers between devices: 441 us -> 424 us  [scatter(): lax.psum_scatter(value, axes, scatter_dimension=0, tiled=True).astype(f32)]
  transfers between devices with their start and end apart: 17 -> 9, of which waited for: 14 -> 9; matrix products, arithmetic and copies ran while one was open for 28% -> 7% of each run, Pallas kernels for 0% -> 2%
where the time goes in v1:
time: 960 us; the launch traced here: 956 us
  waiting for transfers between devices  713 us (74%)
  Pallas kernels  117 us (12%)
  other arithmetic  41.6 us (4%)
  matrix products  39.6 us (4%)
  local copies, waits for them, and re-layouts  23.8 us (2%)
  between operations  14.6 us (2%)
    reduce_scatter x4, waiting for transfers between devices, scatter(): lax.psum_scatter(value, axes, scatter_dimension=0, tiled=True).astype(f32)  424 us
    psum x1, waiting for transfers between devices, per_device(): summed = lax.psum(packed, everyone)  104 us
    all_gather x1, waiting for transfers between devices, per_device(): down_full = lax.all_gather(down_weight.T, ('mlp', 'dp'), axis=0, tiled=True)  65.1 us
    pallas_call x1, Pallas kernels, feed(): pl.pallas_call(lambda *refs: feed_kernel(*refs, chunk=chunk, steps=steps)...  60.9 us
    all_gather x1, waiting for transfers between devices, per_device(): up_full = lax.all_gather(up_weight, ('mlp', 'dp'), axis=0, tiled=True)  57.3 us
    dot_general x6, matrix products, dot(): return lax.dot_general(left, right, dims, preferred_element_type=f32)  37.6 us
    all_gather x1, waiting for transfers between devices, per_device(): lax.all_gather(pair_major(qkv_weight), everyone, axis=0, tiled=True)  35.4 us
    pallas_call x1, Pallas kernels, attend_back(): pl.pallas_call(lambda *refs: attend_back_kernel(*refs, chunk=chunk), grid...  34.4 us
  transfers between devices with their start and end apart: 9, of which 9 were waited for; matrix products, arithmetic and copies ran while one was open for 7% of the time, Pallas kernels for 2%

profile of v1, /device:TPU:0, one launch (start us, length us, event | category | flops | bytes accessed | tf_op | source)
XLA Modules:
  0.0 955.6 jit_solution(1053378717758295062)
XLA Ops:
  15.4 4.2 gather_fusion
  19.6 2.8 fusion.3
  22.5 3.7 convert_reduce_fusion.1
  26.6 5.5 all-gather
  33.3 3.1 bitcast_select_fusion.1.refs_1_
  36.4 2.6 fusion.2
  39.0 35.4 %all-gather.6.cloned.1.call-done = bf16[768,2304]{1,0:T(8,128)(2,1)} async-done(((bf16[24,2304]{1,0:T(8,128)(2,1)}), bf16[768,2304]{1,0:T(8,128)(2,1)}) %all-gather.6.cloned.1.call-update) | async-done | bytes 3538960 | tf_op jit(solution)/shard_map/all_gather | solution.py:314
  74.4 8.3 fusion.refs_0_
  82.7 21.6 %attend.1 = (bf16[1280,768]{1,0:T(8,128)(2,1)S(1)}, f32[1280,128]{1,0:T(8,128)S(1)}) custom-call(bf16[1280,2304]{1,0:T(8,128)(2,1)S(1)} %fusion.refs_0_, bf16[1280,128]{1,0:T(8,128)(2,1)S(1)} %fusion.6.refs_1_.refs_3_, bf16[1280,128]{1,0:T(8,128)(2,1)S(1)} %select_convert_fusion.1.refs_2_.refs_4_), custom_call_target="tpu_custom_call" | custom-call | flops 10066329600 | bytes 7864320 | tf_op jit(solution)/shard_map/attend/pallas_call | solution.py:106
  104.3 2.5 copy-done.1
  106.8 23.5 %all-gather.8.cloned.1.call-done = bf16[768,768]{1,0:T(8,128)(2,1)} async-done(((bf16[24,768]{1,0:T(8,128)(2,1)}), bf16[768,768]{1,0:T(8,128)(2,1)}) %all-gather.8.cloned.1.call-update) | async-done | bytes 1179664 | tf_op jit(solution)/shard_map/all_gather | solution.py:315
  130.3 4.3 fusion.19
  136.5 1.9 add_convert_fusion.refs_0_
  138.4 57.3 %all-gather.10.cloned.1.call-done = bf16[1536,1536]{1,0:T(8,128)(2,1)} async-done(((bf16[48,1536]{1,0:T(8,128)(2,1)}), bf16[1536,1536]{1,0:T(8,128)(2,1)}) %all-gather.10.cloned.1.call-update) | async-done | bytes 4718608 | tf_op jit(solution)/shard_map/all_gather | solution.py:316
  195.7 65.1 %all-gather.12.cloned.1.call-done = bf16[1536,1536]{1,0:T(8,128)(2,1)} async-done(((bf16[48,1536]{1,0:T(8,128)(2,1)}), bf16[1536,1536]{1,0:T(8,128)(2,1)}) %all-gather.12.cloned.1.call-update) | async-done | bytes 4718608 | tf_op jit(solution)/shard_map/all_gather | solution.py:317
  260.8 60.9 %feed.1 = (f32[1280,768]{1,0:T(8,128)}, f32[1280,768]{1,0:T(8,128)}, bf16[2,768,1536]{2,1,0:T(8,128)(2,1)}, bf16[2,768,1536]{2,1,0:T(8,128)(2,1)}, f32[1,3072]{1,0:T(1,128)}) custom-call(bf16[1280,768]{1,0:T(8,128)(2,1)} %add_convert_fusion.refs_0_, bf16[1280,768]{1,0:T(8,128)(2,1)} %bitcast_select_fusion.1.refs_1_, bf16[2,768,1536]{2,1,0:T(8,128)(2,1)} %bitcast.72, ...), custom_call_target="tpu_custom_call" | custom-call | flops 36238786560 | bytes 30670848 | tf_op jit(solution)/shard_map/feed/pallas_call | solution.py:255
  321.7 3.6 multiply_reduce_fusion
  325.6 5.4 fusion.16
  331.0 1.7 convolution_convert_fusion.1.refs_1_
  332.8 34.4 %attend_back.1 = bf16[1280,2304]{1,0:T(8,128)(2,1)S(1)} custom-call(bf16[1280,2304]{1,0:T(8,128)(2,1)} %copy-done.1, bf16[1280,768]{1,0:T(8,128)(2,1)S(1)} %convolution_convert_fusion.1.refs_1_, bf16[1280,768]{1,0:T(8,128)(2,1)S(1)} %get-tuple-element.23.refs_2_, bf16[1280,128]{1,0:T(8,128)(2,1)S(1)} %fusion.6.refs_1_.refs_3_, ...), custom_call_target="tpu_custom_call" | custom-call | flops 25165824000 | bytes 15728640 | tf_op jit(solution)/shard_map/attend_back/pallas_call | solution.py:181
  368.1 3.3 copy-done.6
  371.5 7.4 multiply_reduce_fusion.1
  380.2 6.5 broadcast_select_fusion
  386.7 2.0 fusion.8
  388.7 2.7 concatenate.24
  391.6 4.9 convolution_convert_fusion.2
  396.6 10.9 %convolution_convert_fusion = bf16[768,2304]{1,0:T(8,128)(2,1)} fusion(bf16[1280,2304]{1,0:T(8,128)(2,1)} %copy-done, f32[1280,768]{1,0:T(8,128)} %fusion.2, f32[768]{0:T(1024)S(1)} %convert_element_type.96, f32[768]{0:T(1024)S(1)} %convert_element_type.95, f32[1280]{0:T(1024)S(1)} %rsqrt.20, f32[1280]{0:T(1024)S(1)} %div.27), kind=kOutput, calls=%fused_computation.4 | convolution fusion | flops 4536532992 | bytes 13385728 | tf_op jit(solution)/shard_map/dot_general | solution.py:37
  409.1 104.4 %all-reduce.2.cloned.1.call-done = f32[62,768]{1,0:T(8,128)} async-done(((f32[62,768]{1,0:T(8,128)}), f32[62,768]{1,0:T(8,128)}) %all-reduce.2.cloned.1.call-update) | async-done | bytes 190480 | tf_op jit(solution)/shard_map/psum | solution.py:408
  518.2 97.3 %reduce-scatter.7.cloned.1.call-done = bf16[24,768]{1,0:T(8,128)(2,1)} async-done(((bf16[768,768]{1,0:T(8,128)(2,1)}), bf16[24,768]{1,0:T(8,128)(2,1)}) %reduce-scatter.7.cloned.1.call-update) | async-done | bytes 36880 | tf_op jit(solution)/shard_map/reduce_scatter | solution.py:386
  616.9 106.3 %reduce-scatter.5.cloned.1.call-done = bf16[24,2304]{1,0:T(8,128)(2,1)} async-done(((bf16[768,2304]{1,0:T(8,128)(2,1)}), bf16[24,2304]{1,0:T(8,128)(2,1)}) %reduce-scatter.5.cloned.1.call-update) | async-done | bytes 110608 | tf_op jit(solution)/shard_map/reduce_scatter | solution.py:386
  725.0 109.7 %reduce-scatter.11.cloned.1.call-done = bf16[48,1536]{1,0:T(8,128)(2,1)} async-done(((bf16[1536,1536]{1,0:T(8,128)(2,1)}), bf16[48,1536]{1,0:T(8,128)(2,1)}) %reduce-scatter.11.cloned.1.call-update) | async-done | bytes 147472 | tf_op jit(solution)/shard_map/reduce_scatter | solution.py:386
  836.4 110.9 %reduce-scatter.9.cloned.1.call-done = bf16[48,1536]{1,0:T(8,128)(2,1)} async-done(((bf16[1536,1536]{1,0:T(8,128)(2,1)}), bf16[48,1536]{1,0:T(8,128)(2,1)}) %reduce-scatter.9.cloned.1.call-update) | async-done | bytes 147472 | tf_op jit(solution)/shard_map/reduce_scatter | solution.py:386
  (131 shorter events, 26.9 us)
Async XLA Ops:
  7.2 67.2 %all-gather.6.cloned.1.call-start = ((), (), s32[]{:S(2)}) async-start(), calls=%async_computation.4 | async-start | bytes 3649536 | tf_op jit(solution)/shard_map/all_gather | solution.py:314
  9.1 121.2 %all-gather.8.cloned.1.call-start = ((), (), s32[]{:S(2)}) async-start(), calls=%async_computation.5 | async-start | bytes 1216512 | tf_op jit(solution)/shard_map/all_gather | solution.py:315
  9.9 185.8 %all-gather.10.cloned.1.call-start = ((), (), s32[]{:S(2)}) async-start(), calls=%async_computation.6 | async-start | bytes 4866048 | tf_op jit(solution)/shard_map/all_gather | solution.py:316
  10.6 250.2 %all-gather.12.cloned.1.call-start = ((), (), s32[]{:S(2)}) async-start(), calls=%async_computation.7 | async-start | bytes 4866048 | tf_op jit(solution)/shard_map/all_gather | solution.py:317
  11.2 502.3 %all-reduce.2.cloned.1.call-start = ((), (), s32[]{:S(2)}) async-start(), calls=%async_computation.8 | async-start | bytes 393216 | tf_op jit(solution)/shard_map/psum | solution.py:408
  22.4 3.9 copy-start.11
  22.4 3.9 copy-start.12
  22.4 3.9 copy-start.17
  22.4 3.9 copy-start.18
  22.4 4.1 copy-start.13
  22.4 4.1 copy-start.14
  22.5 4.1 copy-start.15
  22.5 4.1 copy-start.10
  22.5 10.3 %copy-start.16 = (bf16[768]{0:T(1024)(128)(2,1)S(1)}, bf16[768]{0:T(1024)(128)(2,1)}, u32[]{:S(2)}) copy-start(bf16[768]{0:T(1024)(128)(2,1)} %param.37) | copy-start | bytes 4612
  26.5 9.9 %copy-start.4 = (bf16[2,640,768]{2,1,0:T(8,128)(2,1)S(1)}, bf16[2,640,768]{2,1,0:T(8,128)(2,1)}, u32[]{:S(2)}) copy-start(bf16[2,640,768]{2,1,0:T(8,128)(2,1)} %param.19) | copy-start | bytes 5898244
  104.3 2.5 copy-start.1
  134.6 1.9 copy-start.2
  260.8 60.9 %copy-start.3 = (f32[1280,768]{1,0:T(8,128)S(1)}, f32[1280,768]{1,0:T(8,128)}, u32[]{:S(2)}) copy-start(f32[1280,768]{1,0:T(8,128)} %copy-done.2) | copy-start | bytes 11796484
  321.7 3.6 copy-start.5
  321.7 3.9 copy-start.8
  325.6 5.4 copy-start.20
  331.0 1.9 copy-start.7
  332.8 35.3 %copy-start.19 = (bf16[768,2304]{1,0:T(8,128)(2,1)S(1)}, bf16[768,2304]{1,0:T(8,128)(2,1)}, u32[]{:S(2)}) copy-start(bf16[768,2304]{1,0:T(8,128)(2,1)} %all-gather.6.cloned.1.call-done) | copy-start | bytes 10616836
  367.2 11.7 %copy-start = (bf16[1280,2304]{1,0:T(8,128)(2,1)}, bf16[1280,2304]{1,0:T(8,128)(2,1)S(1)}, u32[]{:S(2)}) copy-start(bf16[1280,2304]{1,0:T(8,128)(2,1)S(1)} %attend_back.1) | copy-start | bytes 17694724
  367.2 4.2 copy-start.6
  371.5 8.0 copy-start.9
  391.4 224.1 %reduce-scatter.7.cloned.1.call-start = ((), (), s32[]{:S(2)}) async-start(), calls=%async_computation.10 | async-start | bytes 1216512 | tf_op jit(solution)/shard_map/reduce_scatter | solution.py:386
  396.6 326.6 %reduce-scatter.5.cloned.1.call-start = ((), (), s32[]{:S(2)}) async-start(), calls=%async_computation.9 | async-start | bytes 3649536 | tf_op jit(solution)/shard_map/reduce_scatter | solution.py:386
  407.6 427.1 %reduce-scatter.11.cloned.1.call-start = ((), (), s32[]{:S(2)}) async-start(), calls=%async_computation.12 | async-start | bytes 4866048 | tf_op jit(solution)/shard_map/reduce_scatter | solution.py:386
  408.3 538.9 %reduce-scatter.9.cloned.1.call-start = ((), (), s32[]{:S(2)}) async-start(), calls=%async_computation.11 | async-start | bytes 4866048 | tf_op jit(solution)/shard_map/reduce_scatter | solution.py:386
Sparse Core Ops, SparseCore 0:
  11.5 62.8 all-gather.5
  77.3 52.9 all-gather.7
  133.2 62.4 all-gather.9
  198.4 62.3 all-gather.11
  391.5 121.8 all-reduce.1
  518.4 97.0 reduce-scatter.6
  621.0 102.2 reduce-scatter.4
  728.7 105.9 reduce-scatter.10
  841.1 106.1 reduce-scatter.8
